TPU v7x, 32 devices: a whole 2x2x4 slice. The times are simulated.
32 devices in a mesh: req: 4 (over y, x), seq: 8 (over z, core).
Axes of the slice: x: 2, y: 2, z: 4, core: 2. Of those that a mesh axis runs over, the one named last changes fastest.
Arguments:
- residual: bfloat16 [64, 2048], P(None, ('req', 'seq')), may hold values from -90 to 90
- query_plain: bfloat16 [64, 16, 128], P('req'), may hold values from -6 to 6
- query_rotary: bfloat16 [64, 16, 64], P('req'), may hold values from -110 to 110
- latent_cache: bfloat16 [64, 3072, 512], P('req', 'seq'), may hold values from -9 to 9
- rotary_cache: bfloat16 [64, 64, 3072], P('req', None, 'seq'), may hold values from -4.5 to 4.5
- lengths: int32 [64], P('req'), may hold values from 2 to 3072, as said below
- absorb_key: bfloat16 [16, 128, 512], replicated, may hold values from -0.5 to 0.5
- absorb_value: bfloat16 [16, 512, 128], replicated, may hold values from -0.25 to 0.25
- output_weight: bfloat16 [2048, 2048], P(None, ('req', 'seq')), may hold values from -0.125 to 0.125
- middle_gain: float32 [2048], replicated, may hold values from 0.5 to 1.5
- routes: int32 [64, 6], replicated, may hold values from 0 to 63, all different within a row
- route_weights: float32 [64, 6], replicated, may hold values from 0.05 to 0.45
- gate_weight: bfloat16 [64, 2048, 1408], P('seq', None, 'req'), may hold values from -0.125 to 0.125
- up_weight: bfloat16 [64, 2048, 1408], P('seq', None, 'req'), may hold values from -0.125 to 0.125
- down_weight: bfloat16 [64, 1408, 2048], P('seq', 'req'), may hold values from -0.15625 to 0.15625
- shared_gate: bfloat16 [2048, 2816], P(None, ('req', 'seq')), may hold values from -0.125 to 0.125
- shared_up: bfloat16 [2048, 2816], P(None, ('req', 'seq')), may hold values from -0.125 to 0.125
- shared_down: bfloat16 [2816, 2048], P(('req', 'seq')), may hold values from -0.109375 to 0.109375
- final_gain: float32 [2048], replicated, may hold values from 0.5 to 1.5
- unembed: bfloat16 [102400, 2048], P(('req', 'seq')), may hold values from -0.65115609 to 0.65115609
Outputs:
- layer_out: bfloat16 [64, 2048], P(None, ('req', 'seq'))
- best_logits: float32 [64, 2], replicated
Inputs may be any that keep to these rules, and one draw needn't show every extreme that they name: Request r uses cache positions 0 to lengths[r] - 1, the new token's entry included; in every draw some request's cache is full.
All inputs are finite; a program needn't handle non-finite values.
Results may differ from a plain program's by a relative error of at most 0.0095.
Values may be sent and summed in bfloat16 or wider, within the bound.
A program may use at most 128 MiB of HBM per device.

v0:
```python
import jax
import jax.numpy as jnp
from jax import lax
from jax.sharding import PartitionSpec as P

NEG_FILL = -1e30
NORM_EPS = 1e-06


def combined_all(x, axis, join):
    gathered = jax.tree.map(
        lambda a, kind: lax.all_gather(a.astype(kind), axis),
        x,
        (jnp.bfloat16, jnp.bfloat16, jnp.bfloat16),
    )

    def take(source):
        return jax.tree.map(
            lambda a, own: lax.dynamic_index_in_dim(a, source, 0, False).astype(own.dtype),
            gathered,
            x,
        )

    return lax.fori_loop(
        1, lax.axis_size(axis), lambda source, state: join(state, take(source)), take(0)
    )


def merged_2(x, axis, combine):
    everything = lax.all_gather(x, axis)
    first = everything[0]

    def hop(k, so_far):
        return combine(so_far, everything[k])

    return lax.fori_loop(1, lax.axis_size(axis), hop, first)


def normed(hidden, gain):
    widened = hidden.astype(jnp.float32)
    meansq = jnp.mean(widened * widened, axis=-1, keepdims=True)
    return (widened * lax.rsqrt(meansq + NORM_EPS) * gain).astype(jnp.bfloat16)


def blend(former, latter):
    largest = jnp.maximum(former[0], latter[0])
    former_rescale = jnp.exp(former[0] - largest)
    latter_rescale = jnp.exp(latter[0] - largest)
    totals = former_rescale * former[1] + latter_rescale * latter[1]
    mixes = former_rescale[..., None] * former[2] + latter_rescale[..., None] * latter[2]
    return (largest, totals, mixes)


def best_two(former, latter):
    higher = jnp.maximum(former[:, 0], latter[:, 0])
    lower = jnp.maximum(
        jnp.minimum(former[:, 0], latter[:, 0]), jnp.maximum(former[:, 1], latter[:, 1])
    )
    return jnp.stack([higher, lower], axis=1)


def local(
    residual,
    query_plain,
    query_rotary,
    latent_cache,
    rotary_cache,
    lengths,
    absorb_key,
    absorb_value,
    output_weight,
    middle_gain,
    routes,
    route_weights,
    gate_weight,
    up_weight,
    down_weight,
    shared_gate,
    shared_up,
    shared_down,
    final_gain,
    unembed,
):
    group_rows, head_count, plain_size = query_plain.shape
    block_len = latent_cache.shape[1]
    value_size = absorb_value.shape[2]
    score_scale = (plain_size + query_rotary.shape[2]) ** (-0.5)
    value_wide = absorb_value.astype(jnp.float32)
    query_latent = jnp.einsum(
        "rhn,hnc->rhc", query_plain, absorb_key, preferred_element_type=jnp.float32
    ).astype(jnp.bfloat16)
    scores = jnp.einsum(
        "rhc,rtc->rht", query_latent, latent_cache, preferred_element_type=jnp.float32
    )
    scores = (
        scores
        + jnp.einsum("rhj,rjt->rht", query_rotary, rotary_cache, preferred_element_type=jnp.float32)
    ) * score_scale
    position = lax.axis_index("seq") * block_len + lax.broadcasted_iota(
        jnp.int32, (1, 1, block_len), 2
    )
    usable = position < lengths[:, None, None]
    block_peak = jnp.max(jnp.where(usable, scores, NEG_FILL), axis=2)
    weights = jnp.where(usable, jnp.exp(scores - block_peak[:, :, None]), 0.0).astype(jnp.bfloat16)
    block_total = jnp.sum(weights.astype(jnp.float32), axis=2)
    block_mix = jnp.einsum(
        "rht,rtc->rhc", weights, latent_cache, preferred_element_type=jnp.float32
    )
    merged_peak, merged_total, merged_mix = combined_all(
        (block_peak, block_total, block_mix), "seq", blend
    )
    merged = merged_mix / merged_total[:, :, None]
    merged = jnp.einsum("rhc,hcv->rhv", merged, value_wide, precision=lax.Precision.HIGHEST)
    group_output = merged.astype(jnp.bfloat16).reshape(group_rows, head_count * value_size)
    attn_out = jnp.dot(
        lax.all_gather(group_output, "req", axis=0, tiled=True),
        output_weight,
        preferred_element_type=jnp.float32,
    )
    column_count = residual.shape[1]
    stream_cols = (residual.astype(jnp.float32) + attn_out).astype(jnp.bfloat16)
    stream = lax.all_gather(stream_cols, ("req", "seq"), axis=1, tiled=True)
    expert_in = normed(stream, middle_gain)
    local_count = gate_weight.shape[0]
    expert_index = lax.axis_index("seq") * local_count + lax.broadcasted_iota(
        jnp.int32, (local_count, 1, 1), 0
    )
    route_share = jnp.sum(
        jnp.where(routes[None, :, :] == expert_index, route_weights[None, :, :], 0.0), axis=2
    )
    gate = jnp.einsum("td,edf->etf", expert_in, gate_weight, preferred_element_type=jnp.float32)
    upper = jnp.einsum("td,edf->etf", expert_in, up_weight, preferred_element_type=jnp.float32)
    expert_act = (jax.nn.silu(gate) * upper).astype(jnp.bfloat16)
    expert_back = jnp.einsum(
        "etf,efd->etd", expert_act, down_weight, preferred_element_type=jnp.float32
    )
    shared_gated = jnp.dot(expert_in, shared_gate, preferred_element_type=jnp.float32)
    shared_upper = jnp.dot(expert_in, shared_up, preferred_element_type=jnp.float32)
    shared_act = (jax.nn.silu(shared_gated) * shared_upper).astype(jnp.bfloat16)
    shared_back = jnp.dot(shared_act, shared_down, preferred_element_type=jnp.float32)
    expert_term = jnp.sum(route_share[:, :, None] * expert_back, axis=0) + shared_back
    column_start = lax.axis_index(("req", "seq")) * column_count
    moe = lax.psum(expert_term, ("req", "seq"))
    layer_full = (stream.astype(jnp.float32) + moe).astype(jnp.bfloat16)
    layer_out = lax.dynamic_slice_in_dim(layer_full, column_start, column_count, 1)
    final_in = normed(layer_full, final_gain)
    logits = lax.dot_general(
        final_in, unembed, (((1,), (1,)), ((), ())), preferred_element_type=jnp.float32
    )
    local_best = lax.top_k(logits, 2)[0]
    best_logits = merged_2(local_best, ("req", "seq"), best_two)
    return (layer_out, best_logits)


def solution(mesh):
    in_specs = (
        P(None, ("req", "seq")),
        P("req", None, None),
        P("req", None, None),
        P("req", "seq", None),
        P("req", None, "seq"),
        P("req"),
        P(),
        P(),
        P(None, ("req", "seq")),
        P(),
        P(),
        P(),
        P("seq", None, "req"),
        P("seq", None, "req"),
        P("seq", "req", None),
        P(None, ("req", "seq")),
        P(None, ("req", "seq")),
        P(("req", "seq"), None),
        P(),
        P(("req", "seq"), None),
    )
    out_specs = (P(None, ("req", "seq")), P())
    return jax.shard_map(local, mesh=mesh, in_specs=in_specs, out_specs=out_specs, check_vma=False)
```

profile of v0, /device:TPU:0, one launch (start us, length us, event | category | flops | bytes accessed | tf_op | source)
XLA Modules:
  0.0 327.6 jit_solution(13177338711063554684)
XLA Ops:
  7.3 0.9 broadcast_compare_fusion
  8.2 0.6 copy-done
  8.8 1.9 fusion.6
  10.7 4.5 %fusion.24 = f32[16,16,384]{2,1,0:T(8,128)S(1)} fusion(bf16[16,384,512]{2,1,0:T(8,128)(2,1)} %param.27, bf16[16,16,512]{2,0,1:T(8,128)(2,1)S(1)} %fusion.6), kind=kOutput, calls=%fused_computation.49 | convolution fusion | flops 100663296 | bytes 6946816 | tf_op jit(solution)/shard_map/rhc,rtc->rht/dot_general | solution.py:92
  15.3 0.3 select_reduce_fusion
  15.6 1.7 convolution_convert_fusion.1
  17.7 15.8 %all-gather.1 = bf16[128,16]{1,0:T(8,128)(2,1)S(1)} all-gather(bf16[16,16]{1,0:T(8,128)(2,1)S(1)} %fusion.34), channel_id=3, replica_groups=mesh['req'=4,'seq'=8] {'seq'}, dimensions={0}, use_global_device_ids=true | all-gather | bytes 4608 | tf_op jit(solution)/shard_map/all_gather | solution.py:12
  33.5 14.1 %all-gather = bf16[128,16]{1,0:T(8,128)(2,1)S(1)} all-gather(bf16[16,16]{1,0:T(8,128)(2,1)S(1)} %convert_element_type.122), channel_id=2, replica_groups=mesh['req'=4,'seq'=8] {'seq'}, dimensions={0}, use_global_device_ids=true | all-gather | bytes 4608 | tf_op jit(solution)/shard_map/all_gather | solution.py:12
  47.7 2.0 all-gather.7.cloned.1.call-done
  49.6 1.0 slice_convert_fusion
  50.6 8.3 %while.34 = (s32[]{:T(128)}, f32[16,16]{1,0:T(8,128)S(1)}, f32[16,16]{1,0:T(8,128)S(1)}, f32[16,16,512]{2,1,0:T(8,128)S(1)}, bf16[8,16,16]{2,1,0:T(8,128)(2,1)S(...) while((s32[]{:T(128)}, f32[16,16]{1,0:T(8,128)S(1)}, ...), condition=%wide.region_3.4_spmd, body=%wide.region_2.3_spmd.sunk | while | flops 526341 | bytes 1320087 | solution.py:24
  50.7 1.2 fusion.66
  51.9 1.1 fusion.66
  53.1 1.1 fusion.66
  54.3 1.1 fusion.66
  55.4 1.1 fusion.66
  56.6 1.1 fusion.66
  57.8 1.1 fusion.66
  59.0 2.8 fusion.7
  61.8 8.9 %all_gather.33 = bf16[64,2048]{1,0:T(8,128)(2,1)S(1)} all-gather(bf16[16,2048]{1,0:T(8,128)(2,1)S(1)} %bitcast.66), channel_id=1, replica_groups=mesh['req'=4,'seq'=8] {'req'}, dimensions={0}, use_global_device_ids=true | all-gather | bytes 327680 | tf_op jit(solution)/shard_map/all_gather | solution.py:116
  71.1 41.6 %all_gather.34 = bf16[64,2048]{0,1:T(8,128)(2,1)S(1)} all-gather(bf16[64,64]{0,1:T(8,128)(2,1)S(1)} %copy.44), channel_id=1, replica_groups=mesh['req'=4,'seq'=8] {'req','seq'}, dimensions={1}, use_global_device_ids=true | all-gather | bytes 270336 | tf_op jit(solution)/shard_map/all_gather | solution.py:122
  113.1 0.3 fusion.41
  113.4 7.9 %convolution_bitcast_fusion.1 = f32[8,64,352]{2,1,0:T(8,128)S(1)} fusion(bf16[8,2048,352]{1,2,0:T(8,128)(2,1)} %param.36, bf16[64,2048]{1,0:T(8,128)(2,1)S(1)} %copy.45, f32[2048]{0:T(1024)S(1)} %copy-done.7, f32[64]{0:T(128)S(1)} %add_rsqrt_fusion.1), kind=kOutput, calls=%fused_computation.15 | convolution fusion | flops 738721792 | bytes 12525824 | tf_op jit(solution)/shard_map/td,edf->etf/dot_general | solution.py:131
  121.4 13.4 %multiply_reduce_fusion = f32[64,2048]{1,0:T(8,128)S(1)} fusion(bf16[8,352,2048]{2,1,0:T(8,128)(2,1)} %param.38, f32[8,64]{1,0:T(8,128)S(1)} %select_reduce_fusion.1, bf16[8,2048,352]{1,2,0:T(8,128)(2,1)} %param.37, f32[8,64,352]{2,1,0:T(8,128)S(1)} %convolution_bitcast_fusion.1, bf16[64,2048]{1,0:T(8,128)(2,1)S(1)} %copy.45, f32[2048]{0:T(1024)S(1)} %copy-done.7, ...), kind=kOutput, calls=%fused_computation.12 | convolution fusion | flops 1479966720 | bytes 24586496 | tf_op jit(solution)/shard_map/etf,efd->etd/dot_general | solution.py:134
  134.8 1.4 convolution_add_fusion
  136.3 125.3 %all-reduce.2.cloned.1.call-done = f32[64,2048]{1,0:T(8,128)} async-done(((f32[64,2048]{1,0:T(8,128)}), f32[64,2048]{1,0:T(8,128)}) %all-reduce.2.cloned.1.call-update) | async-done | bytes 524304 | tf_op jit(solution)/shard_map/psum | solution.py:143
  261.6 1.2 fusion.10
  262.8 9.0 %fusion.19 = f32[64,3200]{1,0:T(8,128)S(1)} fusion(bf16[3200,2048]{1,0:T(8,128)(2,1)} %param.43, bf16[64,2048]{1,0:T(8,128)(2,1)S(1)} %get-tuple-element.299, f32[2048]{0:T(1024)S(1)} %copy-done.11, f32[64]{0:T(128)S(1)} %add_rsqrt_fusion), kind=kOutput, calls=%fused_computation.45 | convolution fusion | flops 839385088 | bytes 14196992 | tf_op jit(solution)/shard_map/dot_general | solution.py:147
  271.8 6.6 %top_k.7 = (f32[64,2]{1,0:T(8,128)S(1)}, s32[64,2]{1,0:T(8,128)}) custom-call(f32[64,3200]{1,0:T(8,128)S(1)} %fusion.19), custom_call_target="TopK", called_computations={%compare_greater_than.1.10.clone.clone} | custom-call | tf_op jit(solution)/shard_map/top_k | solution.py:150
  278.4 39.6 %all-gather.4 = f32[32,64,2]{1,2,0:T(2,128)S(1)} all-gather(f32[1,64,2]{1,2,0:T(2,128)S(1)} %bitcast.69), channel_id=5, replica_groups=mesh['req'=4,'seq'=8] {'req','seq'}, dimensions={0}, use_global_device_ids=true | all-gather | bytes 16896 | tf_op jit(solution)/shard_map/all_gather | solution.py:30
  318.0 2.0 while.35
  320.1 0.7 constant_dynamic-slice_fusion
  (150 shorter events, 2.3 us)
Async XLA Ops:
  7.2 1.6 copy-start
  7.2 8.1 %copy-start.8 = (bf16[16,16,64]{2,1,0:T(8,128)(2,1)S(1)}, bf16[16,16,64]{2,1,0:T(8,128)(2,1)}, u32[]{:S(2)}) copy-start(bf16[16,16,64]{2,1,0:T(8,128)(2,1)} %param.26) | copy-start | bytes 98308
  7.2 8.1 %copy-start.3 = (bf16[16,64,384]{2,1,0:T(8,128)(2,1)S(1)}, bf16[16,64,384]{2,1,0:T(8,128)(2,1)}, u32[]{:S(2)}) copy-start(bf16[16,64,384]{2,1,0:T(8,128)(2,1)} %param.28) | copy-start | bytes 2359300
  7.2 42.4 %all-gather.7.cloned.1.call-start = ((), (), s32[]{:S(2)}) async-start(), calls=%async_computation.1 | async-start | bytes 2359296 | tf_op jit(solution)/shard_map/all_gather | solution.py:12
  7.3 8.4 %copy-start.2 = (bf16[16,384,512]{2,1,0:T(8,128)(2,1)S(1)}, bf16[16,384,512]{2,1,0:T(8,128)(2,1)}, u32[]{:S(2)}) copy-start(bf16[16,384,512]{2,1,0:T(8,128)(2,1)} %param.27) | copy-start | bytes 18874372
  15.3 32.3 %copy-start.12 = (f32[64,6]{0,1:T(8,128)S(1)}, f32[64,6]{0,1:T(8,128)}, u32[]{:S(2)}) copy-start(f32[64,6]{0,1:T(8,128)} %param.35) | copy-start | bytes 4612
  15.3 32.3 %copy-start.13 = (s32[64,6]{0,1:T(8,128)S(1)}, s32[64,6]{0,1:T(8,128)}, u32[]{:S(2)}) copy-start(s32[64,6]{0,1:T(8,128)} %param.34) | copy-start | bytes 4612
  17.4 244.2 %all-reduce.2.cloned.1.call-start = ((), (), s32[]{:S(2)}) async-start(), calls=%async_computation | async-start | bytes 1048576 | tf_op jit(solution)/shard_map/psum | solution.py:143
  17.4 53.4 %copy-start.6 = (bf16[2048,64]{0,1:T(8,128)(2,1)S(1)}, bf16[2048,64]{0,1:T(8,128)(2,1)}, u32[]{:S(2)}) copy-start(bf16[2048,64]{0,1:T(8,128)(2,1)} %param.32) | copy-start | bytes 786436
  17.4 53.3 %copy-start.10 = (bf16[64,64]{1,0:T(8,128)(2,1)S(1)}, bf16[64,64]{1,0:T(8,128)(2,1)}, u32[]{:S(2)}) copy-start(bf16[64,64]{1,0:T(8,128)(2,1)} %param.24) | copy-start | bytes 24580
  50.6 62.5 %copy-start.7 = (f32[2048]{0:T(1024)S(1)}, f32[2048]{0:T(1024)}, u32[]{:S(2)}) copy-start(f32[2048]{0:T(1024)} %param.33) | copy-start | bytes 24580
  50.6 62.5 %copy-start.14 = (bf16[2048,88]{0,1:T(8,128)(2,1)S(1)}, bf16[2048,88]{0,1:T(8,128)(2,1)}, u32[]{:S(2)}) copy-start(bf16[2048,88]{0,1:T(8,128)(2,1)} %param.39) | copy-start | bytes 1081348
  121.4 13.4 %copy-start.4 = (bf16[88,2048]{1,0:T(8,128)(2,1)S(1)}, bf16[88,2048]{1,0:T(8,128)(2,1)}, u32[]{:S(2)}) copy-start(bf16[88,2048]{1,0:T(8,128)(2,1)} %param.41) | copy-start | bytes 1081348
  121.4 13.4 %copy-start.5 = (bf16[2048,88]{0,1:T(8,128)(2,1)S(1)}, bf16[2048,88]{0,1:T(8,128)(2,1)}, u32[]{:S(2)}) copy-start(bf16[2048,88]{0,1:T(8,128)(2,1)} %param.40) | copy-start | bytes 1081348
  121.4 141.4 %copy-start.11 = (f32[2048]{0:T(1024)S(1)}, f32[2048]{0:T(1024)}, u32[]{:S(2)}) copy-start(f32[2048]{0:T(1024)} %param.42) | copy-start | bytes 24580
  262.8 58.0 %copy-start.1 = (bf16[16,128,512]{2,1,0:T(8,128)(2,1)S(1)}, bf16[16,128,512]{2,1,0:T(8,128)(2,1)}, u32[]{:S(2)}) copy-start(bf16[16,128,512]{2,1,0:T(8,128)(2,1)} %param.30) | copy-start | bytes 6291460
  320.0 0.7 copy-start.9
Sparse Core Ops, SparseCore 0:
  17.5 32.0 all-gather.6
  136.4 125.1 all-reduce.1
where the time goes:
time: 328 us
  waiting for transfers between devices  127 us (39%)
  blocking collectives  120 us (37%)
  matrix products  43.5 us (13%)
  other arithmetic  18.8 us (6%)
  between operations  14.4 us (4%)
    psum x1, waiting for transfers between devices, local(): moe = lax.psum(expert_term, ('req', 'seq'))  125 us
    all_gather x1, blocking collectives, local(): stream = lax.all_gather(stream_cols, ('req', 'seq'), axis=1, tiled=True)  41.6 us
    all_gather x1, blocking collectives, merged_2(): everything = lax.all_gather(x, axis)  39.6 us
    all_gather x2, blocking collectives, combined_all(): lax.all_gather(a.astype(kind), axis)  29.9 us
    dot_general x1, matrix products, local(): jnp.einsum('etf,efd->etd', expert_act, down_weight, preferred_element_typ...  13.4 us
    dot_general x1, matrix products, local(): lax.dot_general(final_in, unembed, (((1,), (1,)), ((), ())), preferred_el...  8.97 us
    all_gather x1, blocking collectives, local(): lax.all_gather(group_output, 'req', axis=0, tiled=True)  8.95 us
    dot_general x1, matrix products, local(): jnp.einsum('td,edf->etf', expert_in, gate_weight, preferred_element_type=...  7.94 us
  transfers between devices with their start and end apart: 2, of which 2 were waited for; matrix products, arithmetic and copies ran while one was open for 0% of the time, Pallas kernels for 0%

commit v1 on v0

--- a/solution.py
+++ b/solution.py
@@ -2,6 +2,7 @@
 import jax.numpy as jnp
 from jax import lax
 from jax.sharding import PartitionSpec as P
+from jax.lax import psum
 
 NEG_FILL = -1e30
 NORM_EPS = 1e-06
@@ -140,7 +141,9 @@
     shared_back = jnp.dot(shared_act, shared_down, preferred_element_type=jnp.float32)
     expert_term = jnp.sum(route_share[:, :, None] * expert_back, axis=0) + shared_back
     column_start = lax.axis_index(("req", "seq")) * column_count
-    moe = lax.psum(expert_term, ("req", "seq"))
+    moe = expert_term
+    for s in ("seq", "req"):
+        moe = psum(moe, s)
     layer_full = (stream.astype(jnp.float32) + moe).astype(jnp.bfloat16)
     layer_out = lax.dynamic_slice_in_dim(layer_full, column_start, column_count, 1)
     final_in = normed(layer_full, final_gain)

time: 328 us -> 305 us (0.930)
  waiting for transfers between devices: 127 us -> 103 us
    psum x1 -> x2, waiting for transfers between devices: 125 us -> 101 us  [local(): moe = psum(moe, s)]
  transfers between devices with their start and end apart: 2 -> 3, of which waited for: 2 -> 3; matrix products, arithmetic and copies ran while one was open for 0% -> 0% of each run, Pallas kernels for 0% -> 0%
where the time goes in v1:
time: 305 us; the launch traced here: 304 us
  blocking collectives  121 us (40%)
  waiting for transfers between devices  103 us (34%)
  matrix products  43.5 us (14%)
  other arithmetic  18.8 us (6%)
  between operations  14.1 us (5%)
    psum x2, waiting for transfers between devices, local(): moe = psum(moe, s)  101 us
    all_gather x1, blocking collectives, local(): stream = lax.all_gather(stream_cols, ('req', 'seq'), axis=1, tiled=True)  41.6 us
    all_gather x1, blocking collectives, merged_2(): everything = lax.all_gather(x, axis)  40.6 us
    all_gather x2, blocking collectives, combined_all(): lax.all_gather(a.astype(kind), axis)  29.9 us
    dot_general x1, matrix products, local(): jnp.einsum('etf,efd->etd', expert_act, down_weight, preferred_element_typ...  13.4 us
    dot_general x1, matrix products, local(): lax.dot_general(final_in, unembed, (((1,), (1,)), ((), ())), preferred_el...  8.97 us
    all_gather x1, blocking collectives, local(): lax.all_gather(group_output, 'req', axis=0, tiled=True)  8.95 us
    dot_general x1, matrix products, local(): jnp.einsum('td,edf->etf', expert_in, gate_weight, preferred_element_type=...  7.94 us
  transfers between devices with their start and end apart: 3, of which 3 were waited for; matrix products, arithmetic and copies ran while one was open for 0% of the time, Pallas kernels for 0%

profile of v1, /device:TPU:0, one launch (start us, length us, event | category | flops | bytes accessed | tf_op | source)
XLA Modules:
  0.0 304.1 jit_solution(14796027594427956927)
XLA Ops:
  7.3 0.9 broadcast_compare_fusion
  8.2 0.6 copy-done
  8.8 1.9 fusion.6
  10.7 4.5 %fusion.24 = f32[16,16,384]{2,1,0:T(8,128)S(1)} fusion(bf16[16,384,512]{2,1,0:T(8,128)(2,1)} %param.27, bf16[16,16,512]{2,0,1:T(8,128)(2,1)S(1)} %fusion.6), kind=kOutput, calls=%fused_computation.49 | convolution fusion | flops 100663296 | bytes 6946816 | tf_op jit(solution)/shard_map/rhc,rtc->rht/dot_general | solution.py:93
  15.3 0.3 select_reduce_fusion
  15.6 1.7 convolution_convert_fusion.1
  17.7 15.8 %all-gather.1 = bf16[128,16]{1,0:T(8,128)(2,1)S(1)} all-gather(bf16[16,16]{1,0:T(8,128)(2,1)S(1)} %fusion.34), channel_id=3, replica_groups=mesh['req'=4,'seq'=8] {'seq'}, dimensions={0}, use_global_device_ids=true | all-gather | bytes 4608 | tf_op jit(solution)/shard_map/all_gather | solution.py:13
  33.5 14.1 %all-gather = bf16[128,16]{1,0:T(8,128)(2,1)S(1)} all-gather(bf16[16,16]{1,0:T(8,128)(2,1)S(1)} %convert_element_type.122), channel_id=2, replica_groups=mesh['req'=4,'seq'=8] {'seq'}, dimensions={0}, use_global_device_ids=true | all-gather | bytes 4608 | tf_op jit(solution)/shard_map/all_gather | solution.py:13
  47.7 2.0 all-gather.7.cloned.1.call-done
  49.6 1.0 slice_convert_fusion
  50.6 8.3 %while.34 = (s32[]{:T(128)}, f32[16,16]{1,0:T(8,128)S(1)}, f32[16,16]{1,0:T(8,128)S(1)}, f32[16,16,512]{2,1,0:T(8,128)S(1)}, bf16[8,16,16]{2,1,0:T(8,128)(2,1)S(...) while((s32[]{:T(128)}, f32[16,16]{1,0:T(8,128)S(1)}, ...), condition=%wide.region_3.4_spmd, body=%wide.region_2.3_spmd.sunk | while | flops 526341 | bytes 1320087 | solution.py:25
  50.7 1.2 fusion.66
  51.9 1.1 fusion.66
  53.1 1.1 fusion.66
  54.3 1.1 fusion.66
  55.4 1.1 fusion.66
  56.6 1.1 fusion.66
  57.8 1.1 fusion.66
  59.0 2.8 fusion.7
  61.8 8.9 %all_gather.33 = bf16[64,2048]{1,0:T(8,128)(2,1)S(1)} all-gather(bf16[16,2048]{1,0:T(8,128)(2,1)S(1)} %bitcast.66), channel_id=1, replica_groups=mesh['req'=4,'seq'=8] {'req'}, dimensions={0}, use_global_device_ids=true | all-gather | bytes 327680 | tf_op jit(solution)/shard_map/all_gather | solution.py:117
  71.1 41.6 %all_gather.34 = bf16[64,2048]{0,1:T(8,128)(2,1)S(1)} all-gather(bf16[64,64]{0,1:T(8,128)(2,1)S(1)} %copy.44), channel_id=1, replica_groups=mesh['req'=4,'seq'=8] {'req','seq'}, dimensions={1}, use_global_device_ids=true | all-gather | bytes 270336 | tf_op jit(solution)/shard_map/all_gather | solution.py:123
  113.4 7.9 %convolution_bitcast_fusion.1 = f32[8,64,352]{2,1,0:T(8,128)S(1)} fusion(bf16[8,2048,352]{1,2,0:T(8,128)(2,1)} %param.36, bf16[64,2048]{1,0:T(8,128)(2,1)S(1)} %copy.45, f32[2048]{0:T(1024)S(1)} %copy-done.7, f32[64]{0:T(128)S(1)} %add_rsqrt_fusion.1), kind=kOutput, calls=%fused_computation.15 | convolution fusion | flops 738721792 | bytes 12525824 | tf_op jit(solution)/shard_map/td,edf->etf/dot_general | solution.py:132
  121.4 13.4 %multiply_reduce_fusion = f32[64,2048]{1,0:T(8,128)S(1)} fusion(bf16[8,352,2048]{2,1,0:T(8,128)(2,1)} %param.38, f32[8,64]{1,0:T(8,128)S(1)} %select_reduce_fusion.1, bf16[8,2048,352]{1,2,0:T(8,128)(2,1)} %param.37, f32[8,64,352]{2,1,0:T(8,128)S(1)} %convolution_bitcast_fusion.1, bf16[64,2048]{1,0:T(8,128)(2,1)S(1)} %copy.45, f32[2048]{0:T(1024)S(1)} %copy-done.7, ...), kind=kOutput, calls=%fused_computation.12 | convolution fusion | flops 1479966720 | bytes 24586496 | tf_op jit(solution)/shard_map/etf,efd->etd/dot_general | solution.py:135
  134.8 1.4 convolution_add_fusion
  136.3 53.5 %all-reduce.3.cloned.1.call-done = f32[64,2048]{1,0:T(8,128)} async-done(((f32[64,2048]{1,0:T(8,128)}), f32[64,2048]{1,0:T(8,128)}) %all-reduce.3.cloned.1.call-update) | async-done | bytes 524304 | tf_op jit(solution)/shard_map/psum | solution.py:146
  189.8 47.6 %all-reduce.5.cloned.1.call-done = f32[64,2048]{1,0:T(8,128)} async-done(((f32[64,2048]{1,0:T(8,128)}), f32[64,2048]{1,0:T(8,128)}) %all-reduce.5.cloned.1.call-update) | async-done | bytes 524304 | tf_op jit(solution)/shard_map/psum | solution.py:146
  237.4 1.2 fusion.10
  238.7 9.0 %fusion.19 = f32[64,3200]{1,0:T(8,128)S(1)} fusion(bf16[3200,2048]{1,0:T(8,128)(2,1)} %param.43, bf16[64,2048]{1,0:T(8,128)(2,1)S(1)} %get-tuple-element.299, f32[2048]{0:T(1024)S(1)} %copy-done.11, f32[64]{0:T(128)S(1)} %add_rsqrt_fusion), kind=kOutput, calls=%fused_computation.45 | convolution fusion | flops 839385088 | bytes 14196992 | tf_op jit(solution)/shard_map/dot_general | solution.py:150
  247.6 6.6 %top_k.7 = (f32[64,2]{1,0:T(8,128)S(1)}, s32[64,2]{1,0:T(8,128)}) custom-call(f32[64,3200]{1,0:T(8,128)S(1)} %fusion.19), custom_call_target="TopK", called_computations={%compare_greater_than.1.11.clone.clone} | custom-call | tf_op jit(solution)/shard_map/top_k | solution.py:153
  254.3 40.6 %all-gather.4 = f32[32,64,2]{1,2,0:T(2,128)S(1)} all-gather(f32[1,64,2]{1,2,0:T(2,128)S(1)} %bitcast.69), channel_id=5, replica_groups=mesh['req'=4,'seq'=8] {'req','seq'}, dimensions={0}, use_global_device_ids=true | all-gather | bytes 16896 | tf_op jit(solution)/shard_map/all_gather | solution.py:31
  294.9 2.0 while.35
  296.9 0.7 constant_dynamic-slice_fusion
  (153 shorter events, 2.6 us)
Async XLA Ops:
  7.2 1.6 copy-start
  7.2 8.1 %copy-start.8 = (bf16[16,16,64]{2,1,0:T(8,128)(2,1)S(1)}, bf16[16,16,64]{2,1,0:T(8,128)(2,1)}, u32[]{:S(2)}) copy-start(bf16[16,16,64]{2,1,0:T(8,128)(2,1)} %param.26) | copy-start | bytes 98308
  7.2 8.1 %copy-start.3 = (bf16[16,64,384]{2,1,0:T(8,128)(2,1)S(1)}, bf16[16,64,384]{2,1,0:T(8,128)(2,1)}, u32[]{:S(2)}) copy-start(bf16[16,64,384]{2,1,0:T(8,128)(2,1)} %param.28) | copy-start | bytes 2359300
  7.2 42.4 %all-gather.7.cloned.1.call-start = ((), (), s32[]{:S(2)}) async-start(), calls=%async_computation.2 | async-start | bytes 2359296 | tf_op jit(solution)/shard_map/all_gather | solution.py:13
  7.3 8.4 %copy-start.2 = (bf16[16,384,512]{2,1,0:T(8,128)(2,1)S(1)}, bf16[16,384,512]{2,1,0:T(8,128)(2,1)}, u32[]{:S(2)}) copy-start(bf16[16,384,512]{2,1,0:T(8,128)(2,1)} %param.27) | copy-start | bytes 18874372
  15.3 32.3 %copy-start.12 = (f32[64,6]{0,1:T(8,128)S(1)}, f32[64,6]{0,1:T(8,128)}, u32[]{:S(2)}) copy-start(f32[64,6]{0,1:T(8,128)} %param.35) | copy-start | bytes 4612
  15.3 32.3 %copy-start.13 = (s32[64,6]{0,1:T(8,128)S(1)}, s32[64,6]{0,1:T(8,128)}, u32[]{:S(2)}) copy-start(s32[64,6]{0,1:T(8,128)} %param.34) | copy-start | bytes 4612
  17.4 172.4 %all-reduce.3.cloned.1.call-start = ((), (), s32[]{:S(2)}) async-start(), calls=%async_computation | async-start | bytes 1048576 | tf_op jit(solution)/shard_map/psum | solution.py:146
  17.4 53.4 %copy-start.6 = (bf16[2048,64]{0,1:T(8,128)(2,1)S(1)}, bf16[2048,64]{0,1:T(8,128)(2,1)}, u32[]{:S(2)}) copy-start(bf16[2048,64]{0,1:T(8,128)(2,1)} %param.32) | copy-start | bytes 786436
  17.4 53.3 %copy-start.10 = (bf16[64,64]{1,0:T(8,128)(2,1)S(1)}, bf16[64,64]{1,0:T(8,128)(2,1)}, u32[]{:S(2)}) copy-start(bf16[64,64]{1,0:T(8,128)(2,1)} %param.24) | copy-start | bytes 24580
  50.6 62.5 %copy-start.7 = (f32[2048]{0:T(1024)S(1)}, f32[2048]{0:T(1024)}, u32[]{:S(2)}) copy-start(f32[2048]{0:T(1024)} %param.33) | copy-start | bytes 24580
  50.6 62.5 %copy-start.14 = (bf16[2048,88]{0,1:T(8,128)(2,1)S(1)}, bf16[2048,88]{0,1:T(8,128)(2,1)}, u32[]{:S(2)}) copy-start(bf16[2048,88]{0,1:T(8,128)(2,1)} %param.39) | copy-start | bytes 1081348
  121.4 13.4 %copy-start.4 = (bf16[88,2048]{1,0:T(8,128)(2,1)S(1)}, bf16[88,2048]{1,0:T(8,128)(2,1)}, u32[]{:S(2)}) copy-start(bf16[88,2048]{1,0:T(8,128)(2,1)} %param.41) | copy-start | bytes 1081348
  121.4 13.4 %copy-start.5 = (bf16[2048,88]{0,1:T(8,128)(2,1)S(1)}, bf16[2048,88]{0,1:T(8,128)(2,1)}, u32[]{:S(2)}) copy-start(bf16[2048,88]{0,1:T(8,128)(2,1)} %param.40) | copy-start | bytes 1081348
  121.4 117.3 %copy-start.11 = (f32[2048]{0:T(1024)S(1)}, f32[2048]{0:T(1024)}, u32[]{:S(2)}) copy-start(f32[2048]{0:T(1024)} %param.42) | copy-start | bytes 24580
  136.3 101.2 %all-reduce.5.cloned.1.call-start = ((), (), s32[]{:S(2)}) async-start(), calls=%async_computation.1 | async-start | bytes 1048576 | tf_op jit(solution)/shard_map/psum | solution.py:146
  238.6 58.9 %copy-start.1 = (bf16[16,128,512]{2,1,0:T(8,128)(2,1)S(1)}, bf16[16,128,512]{2,1,0:T(8,128)(2,1)}, u32[]{:S(2)}) copy-start(bf16[16,128,512]{2,1,0:T(8,128)(2,1)} %param.30) | copy-start | bytes 6291460
  296.9 0.7 copy-start.9
Sparse Core Ops, SparseCore 0:
  17.5 32.0 all-gather.6
  136.4 53.3 all-reduce.2
  193.1 44.3 all-reduce.4
